TPU v7x, 128 devices: a whole 4x4x4 slice. The times are simulated.
128 devices in a mesh: dp: 32 (over x, z, core), rep: 4 (over y).
Axes of the slice: x: 4, y: 4, z: 4, core: 2. Of those that a mesh axis runs over, the one named last changes fastest.
Arguments:
- events: bfloat16 [65536, 512], P(('dp', 'rep')), may hold values from -6 to 6
- grad_out: bfloat16 [65536, 512], P(('dp', 'rep')), may hold values from -15 to 15
- w_uvqk: bfloat16 [512, 2048], replicated, may hold values from -0.25 to 0.25
- w_out: bfloat16 [512, 512], replicated, may hold values from -0.25 to 0.25
- send_place: int32 [128, 512], P(('dp', 'rep')), may hold values from 0 to 1023, as said below
- send_counts: int32 [128, 32], P(('dp', 'rep')), may hold values from 0 to 32, as said below
- user_ids: int32 [128, 512], P(('dp', 'rep')), may hold values from 0 to 15, never falling along the last dimension, each value on 1 to 256 neighbouring positions
Outputs:
- grad_events: bfloat16 [65536, 512], P(('dp', 'rep'))
- grad_w_uvqk: float32 [512, 2048], P(None, 'dp')
- grad_w_out: float32 [512, 512], P(None, 'dp')
Inputs may be any that keep to these rules, and one draw needn't show every extreme that they name: `send_counts`: row d * 4 + r gives, for each owner o of group r, how many events device (d, r) sends there; each row sums to 512, and the counts one owner receives from the 32 devices of its group also sum to 512. `send_place`: an event bound for owner o has place o * 32 + j, where j runs from 0 to that owner's count minus 1 over the device's events bound for o; each place at most once on a device. `user_ids`: each row lists an owner's users in the owner's order of events; ids never fall.
All inputs are finite; a program needn't handle non-finite values.
Results may differ from a plain program's by a relative error of at most 0.02.
Values may be sent and summed in bfloat16 or wider, within the bound.
A program may use at most 192 MiB of HBM per device.

v0:
```python
import jax
import jax.numpy as jnp
from jax import lax
from jax.sharding import PartitionSpec as P

HEADS = 8
EPSILON = 1e-05


def normalized_row_block(values):
    center = values - jnp.mean(values, axis=-1, keepdims=True)
    spread = jnp.mean(center * center, axis=-1, keepdims=True)
    return center * lax.rsqrt(spread + EPSILON)


def hstu_layer(event_row_block, input_weight_matrix, weight_out, allowed):
    width = weight_out.shape[0]
    count = event_row_block.shape[0]
    head_size = width // HEADS
    normalized_input = normalized_row_block(event_row_block.astype(jnp.float32)).astype(
        jnp.bfloat16
    )
    activation_value = jax.nn.silu(
        jnp.dot(normalized_input, input_weight_matrix, preferred_element_type=jnp.float32)
    ).astype(jnp.bfloat16)
    gate_u = activation_value[:, :width]
    values = activation_value[:, width : 2 * width].reshape(count, HEADS, head_size)
    queries = activation_value[:, 2 * width : 3 * width].reshape(count, HEADS, head_size)
    keys = activation_value[:, 3 * width :].reshape(count, HEADS, head_size)
    scores = jnp.einsum(
        "qhd,khd->hqk", queries, keys, preferred_element_type=jnp.float32
    ) * head_size ** (-0.5)
    weights = (jax.nn.silu(scores) * allowed[None]).astype(jnp.bfloat16)
    attended = jnp.einsum(
        "hqk,khd->qhd", weights, values, preferred_element_type=jnp.float32
    ).reshape(count, width)
    gated = (normalized_row_block(attended) * gate_u.astype(jnp.float32)).astype(jnp.bfloat16)
    return event_row_block.astype(jnp.float32) + jnp.dot(
        gated, weight_out, preferred_element_type=jnp.float32
    )


def owner_grads(event_row_block, cotangent, input_weight_matrix, weight_out, allowed):
    result, pullback = jax.vjp(
        lambda first, second, third: hstu_layer(first, second, third, allowed),
        event_row_block,
        input_weight_matrix,
        weight_out,
    )
    return pullback(cotangent.astype(jnp.float32))


def on_device(events, grad_out, w_uvqk, w_out, send_place, send_counts, user_ids):
    owners = lax.axis_size("dp")
    owned = events.shape[0]
    width = events.shape[1]
    capacity = 2 * owned // owners
    places_out = send_place[0]
    send_rows = jnp.zeros((owners * capacity, width), jnp.bfloat16).at[places_out].set(events)
    send_grads = jnp.zeros((owners * capacity, width), jnp.bfloat16).at[places_out].set(grad_out)
    recv_rows, recv_grads = (
        lax.all_to_all(send_rows, "dp", split_axis=0, concat_axis=0, tiled=True),
        lax.all_to_all(send_grads, "dp", split_axis=0, concat_axis=0, tiled=True),
    )
    count_table = lax.all_gather(send_counts, "dp", axis=0, tiled=True)
    own_index = lax.axis_index("dp")
    counts_in = lax.dynamic_slice_in_dim(count_table, own_index, 1, 1)[:, 0]
    users = user_ids[0]
    target_positions = jnp.arange(owners * capacity, dtype=jnp.int32)
    source = target_positions // capacity
    within = target_positions - source * capacity
    starts = jnp.cumsum(counts_in) - counts_in
    onehot = (jnp.arange(owners, dtype=jnp.int32)[None, :] == source[:, None]).astype(jnp.int32)
    count_at = jnp.sum(onehot * counts_in[None, :], axis=1)
    starting_offset = jnp.sum(onehot * starts[None, :], axis=1)
    valid = within < count_at
    position = jnp.minimum(starting_offset + within, owned - 1)
    slot_users = jnp.take(users, position)
    allowed = (
        valid[:, None]
        & valid[None, :]
        & (slot_users[:, None] == slot_users[None, :])
        & (target_positions[None, :] <= target_positions[:, None])
    ).astype(jnp.float32)
    grad_rows, grad_in, grad_outw = owner_grads(recv_rows, recv_grads, w_uvqk, w_out, allowed)
    returned = lax.all_to_all(grad_rows, "dp", split_axis=0, concat_axis=0, tiled=True)
    grad_events = jnp.take(returned, places_out, axis=0)
    grad_in = grad_in.astype(jnp.float32)
    grad_outw = grad_outw.astype(jnp.float32)
    part_in, part_out = (
        lax.psum_scatter(
            grad_in.astype(jnp.bfloat16), "dp", scatter_dimension=1, tiled=True
        ).astype(jnp.float32),
        lax.psum_scatter(
            grad_outw.astype(jnp.bfloat16), "dp", scatter_dimension=1, tiled=True
        ).astype(jnp.float32),
    )
    share_in, share_out = (
        lax.psum(part_in.astype(jnp.bfloat16), "rep").astype(jnp.float32),
        lax.psum(part_out.astype(jnp.bfloat16), "rep").astype(jnp.float32),
    )
    return (grad_events, share_in, share_out)


def solution(mesh):
    return jax.shard_map(
        on_device,
        mesh=mesh,
        in_specs=(
            P(("dp", "rep"), None),
            P(("dp", "rep"), None),
            P(),
            P(),
            P(("dp", "rep"), None),
            P(("dp", "rep"), None),
            P(("dp", "rep"), None),
        ),
        out_specs=(P(("dp", "rep"), None), P(None, "dp"), P(None, "dp")),
        check_vma=False,
    )
```

profile of v0, /device:TPU:0, one launch (start us, length us, event | category | flops | bytes accessed | tf_op | source)
XLA Modules:
  0.0 388.2 jit_solution(12523036387752850072)
XLA Ops:
  7.2 0.8 compare_select_fusion.1
  8.0 4.0 %scatter_custom_fusion.1 = bf16[1024,512]{1,0:T(8,128)(2,1)} fusion(s32[512]{0:T(512)S(1)} %bitcast.106, bf16[512,512]{1,0:T(8,128)(2,1)} %param.7, bf16[]{:T(256)} %constant.83.clone.1), kind=kCustom, calls=%fused_computation.50 | custom fusion | bytes 1049088 | tf_op jit(solution)/shard_map/scatter | solution.py:59
  12.0 8.3 %all-to-all-start.1 = ((bf16[32,32,512]{2,1,0:T(8,128)(2,1)}), bf16[32,32,512]{2,1,0:T(8,128)(2,1)S(1)}, u32[]{:S(2)}, u32[]{:S(2)}) async-start(bf16[32,32,512]{2,1,0:T(8,128)(2,1)} %bitcast.95), calls=%async_computation.1 | async-start | bytes 2097152 | tf_op jit(solution)/shard_map/all_to_all | solution.py:62
  20.3 29.8 %all-gather = s32[32,1,32]{2,1,0:T(1,128)S(1)} all-gather(s32[1,1,32]{2,1,0:T(1,128)} %bitcast.110), channel_id=1, replica_groups=mesh['dp'=32,'rep'=4] {'dp'}, dimensions={0}, use_global_device_ids=true | all-gather | bytes 4224 | tf_op jit(solution)/shard_map/all_gather | solution.py:65
  50.1 0.7 fusion.27
  50.8 0.1 reduce-window.8
  50.9 0.1 reduce.6
  51.0 0.1 select_reduce_fusion.1
  51.1 4.0 %scatter_custom_fusion = bf16[1024,512]{1,0:T(8,128)(2,1)} fusion(s32[512]{0:T(512)S(1)} %bitcast.107, bf16[512,512]{1,0:T(8,128)(2,1)} %param.8, bf16[]{:T(256)} %constant.83.clone.1), kind=kCustom, calls=%fused_computation.52 | custom fusion | bytes 1049088 | tf_op jit(solution)/shard_map/scatter | solution.py:60
  55.1 6.9 %gather_fusion = s32[1024]{0:T(1024)S(1)} fusion(s32[512]{0:T(512)S(1)} %bitcast.87, s32[1024]{0:T(1024)S(1)} %broadcast_clamp_fusion), kind=kCustom, calls=%fused_computation | custom fusion | bytes 12288 | tf_op jit(solution)/shard_map/jit(_take)/gather | solution.py:78
  62.0 2.9 fusion.6
  65.0 6.0 %all-to-all-start = ((bf16[32,32,512]{2,1,0:T(8,128)(2,1)}), bf16[32,32,512]{2,1,0:T(8,128)(2,1)}, u32[]{:S(2)}, u32[]{:S(2)}) async-start(bf16[32,32,512]{2,1,0:T(8,128)(2,1)} %bitcast.96), calls=%async_computation | async-start | bytes 2097152 | tf_op jit(solution)/shard_map/all_to_all | solution.py:63
  70.9 0.3 reduce-scatter.5.cloned.1.call-start
  71.3 0.2 convert_reduce_fusion
  71.5 0.1 div.65
  71.6 0.5 multiply_reduce_fusion.1
  72.1 0.1 add.153
  72.2 0.3 multiply_convert_fusion.2
  72.6 5.7 %multiply_convert_fusion.1 = (bf16[1024,2048]{0,1:T(8,128)(2,1)S(1)}, f32[1024,2048]{0,1:T(8,128)}) fusion(bf16[1024,512]{1,0:T(8,128)(2,1)S(1)} %multiply_convert_fusion.2, bf16[512,2048]{1,0:T(8,128)(2,1)S(1)} %copy-done), kind=kOutput, calls=%fused_computation.15 | convolution fusion | flops 2157969408 | bytes 15728640 | tf_op jit(solution)/shard_map/jvp()/dot_general | solution.py:24
  78.3 1.9 copy-done.5
  80.2 1.8 fusion.28
  82.0 21.5 %multiply_convert_fusion = (bf16[8,1024,1024]{2,1,0:T(8,128)(2,1)}, f32[8,1024,1024]{2,1,0:T(8,128)}) fusion(f32[1024,1024]{1,0:T(8,128)} %fusion.6, bf16[1024,8,64]{0,2,1:T(8,128)(2,1)S(1)} %bitcast.90, bf16[1024,8,64]{0,2,1:T(8,128)(2,1)} %bitcast.101), kind=kOutput, calls=%fused_computation.8 | convolution fusion | flops 1132462080 | bytes 56623104 | tf_op jit(solution)/shard_map/jvp(qhd,khd->hqk)/dot_general | solution.py:30
  103.5 12.7 %fusion.29 = (f32[1024]{0:T(1024)S(1)}, f32[8,64,1024]{2,1,0:T(8,128)}) fusion(bf16[1024,8,64]{0,2,1:T(8,128)(2,1)} %bitcast.98, bf16[8,1024,1024]{2,1,0:T(8,128)(2,1)} %get-tuple-element.17), kind=kOutput, calls=%fused_computation.96 | convolution fusion | flops 1074265088 | bytes 19927040 | tf_op jit(solution)/shard_map/jvp(hqk,khd->qhd)/dot_general | solution.py:34
  116.1 1.8 fusion.11
  118.0 3.2 multiply_reduce_fusion
  121.2 4.4 %fusion.8 = (bf16[1024,512]{0,1:T(8,128)(2,1)S(1)}, f32[1024]{0:T(1024)S(1)}, bf16[1024,512]{0,1:T(8,128)(2,1)}) fusion(f32[8,64,1024]{2,1,0:T(8,128)} %get-tuple-element.20, f32[1024]{0:T(1024)S(1)} %broadcast_multiply_fusion.1, f32[1024]{0:T(1024)S(1)} %get-tuple-element.14, bf16[1024,2048]{0,1:T(8,128)(2,1)} %copy-done.5, f32[1024]{0:T(1024)S(1)} %get-tuple-element.13, ...), kind=kLoop, calls=%fused_computation.29 | loop fusion | flops 7339008 | bytes 6307840 | tf_op jit(solution)/shard_map/jvp()/convert_element_type | solution.py:37
  125.6 2.6 broadcast_add_fusion
  128.2 4.0 %fusion.33 = bf16[8,64,1024]{2,1,0:T(8,128)(2,1)} fusion(bf16[8,64,1024]{2,1,0:T(8,128)(2,1)S(1)} %bitcast.93, bf16[8,1024,1024]{2,1,0:T(8,128)(2,1)S(1)} %copy-done.2), kind=kOutput, calls=%fused_computation.100 | convolution fusion | flops 1073741824 | bytes 18874368 | tf_op jit(solution)/shard_map/transpose(jvp(hqk,khd->qhd))/dot_general | solution.py:34
  132.2 23.7 %fusion.2 = bf16[8,1024,1024]{2,1,0:T(8,128)(2,1)} fusion(f32[8,1024,1024]{2,1,0:T(8,128)} %get-tuple-element.18, f32[1024,1024]{1,0:T(8,128)S(1)} %copy-done.8, bf16[8,64,1024]{2,1,0:T(8,128)(2,1)S(1)} %bitcast.94, bf16[1024,8,64]{0,2,1:T(8,128)(2,1)S(1)} %bitcast.99), kind=kOutput, calls=%fused_computation.7 | convolution fusion | flops 1191182336 | bytes 56623104 | tf_op jit(solution)/shard_map/transpose(jvp(hqk,khd->qhd))/dot_general | solution.py:34
  155.9 9.8 %fusion.31 = bf16[8,1024,64]{1,2,0:T(8,128)(2,1)} fusion(bf16[8,1024,1024]{2,1,0:T(8,128)(2,1)} %fusion.2, bf16[1024,8,64]{0,2,1:T(8,128)(2,1)S(1)} %bitcast.102), kind=kOutput, calls=%fused_computation.98 | convolution fusion | flops 1073741824 | bytes 18874368 | tf_op jit(solution)/shard_map/transpose(jvp(qhd,khd->hqk))/dot_general | solution.py:30
  165.8 7.5 %fusion.32 = bf16[8,1024,64]{1,2,0:T(8,128)(2,1)S(1)} fusion(bf16[8,1024,1024]{2,1,0:T(8,128)(2,1)} %fusion.2, bf16[1024,8,64]{0,2,1:T(8,128)(2,1)S(1)} %bitcast.91), kind=kOutput, calls=%fused_computation.99 | convolution fusion | flops 1073741824 | bytes 18874368 | tf_op jit(solution)/shard_map/transpose(jvp(qhd,khd->hqk))/dot_general | solution.py:30
  173.2 2.8 convolution_convert_fusion.6
  176.1 6.4 %fusion.3 = bf16[1024,2048]{0,1:T(8,128)(2,1)S(1)} fusion(f32[1024,2048]{0,1:T(8,128)} %get-tuple-element.16, bf16[1024,512]{0,1:T(8,128)(2,1)} %get-tuple-element.12, bf16[1024,512]{0,1:T(8,128)(2,1)} %bitcast.92, bf16[1024,512]{0,1:T(8,128)(2,1)} %bitcast.100, bf16[1024,512]{0,1:T(8,128)(2,1)S(1)} %bitcast.89), kind=kLoop, calls=%fused_computation.13 | loop fusion | flops 37748736 | bytes 16777216 | tf_op jit(solution)/shard_map/transpose(jvp(jit(silu)))/add_any | solution.py:23
  182.5 1.9 copy-done.9
  184.4 3.7 fusion.30
  188.2 4.9 %fusion.9 = (f32[1024]{0:T(1024)S(1)}, bf16[1024,512]{1,0:T(8,128)(2,1)S(1)}) fusion(bf16[32,32,512]{2,1,0:T(8,128)(2,1)S(1)} %copy-done.4, f32[1024]{0:T(1024)S(1)} %copy-done.16, bf16[1024,2048]{0,1:T(8,128)(2,1)} %copy-done.9, bf16[512,2048]{1,0:T(8,128)(2,1)S(1)} %copy-done), kind=kOutput, calls=%fused_computation.30 | convolution fusion | flops 2150104064 | bytes 8396800 | tf_op jit(solution)/shard_map/transpose(jvp())/dot_general | solution.py:24
  193.1 1.0 fusion.12
  194.2 2.8 fusion.13
  197.0 7.3 %all-to-all-start.2 = ((bf16[32,32,512]{2,1,0:T(8,128)(2,1)}), bf16[32,32,512]{2,1,0:T(8,128)(2,1)S(1)}, u32[]{:S(2)}, u32[]{:S(2)}) async-start(bf16[32,32,512]{2,1,0:T(8,128)(2,1)} %bitcast.97), calls=%async_computation.2 | async-start | bytes 2097152 | tf_op jit(solution)/shard_map/all_to_all | solution.py:86
  204.3 0.0 all-reduce.6.cloned.1.call-start
  204.4 50.9 %reduce-scatter.5.cloned.1.call-done = bf16[512,16]{0,1:T(8,128)(2,1)} async-done(((bf16[512,512]{0,1:T(8,128)(2,1)}), bf16[512,16]{0,1:T(8,128)(2,1)}) %reduce-scatter.5.cloned.1.call-update) | async-done | bytes 16400 | tf_op jit(solution)/shard_map/reduce_scatter | solution.py:94
  255.3 17.5 %psum.15 = bf16[512,16]{0,1:T(8,128)(2,1)S(1)} all-reduce(bf16[512,16]{0,1:T(8,128)(2,1)} %reduce-scatter.5.cloned.1.call-done), channel_id=1, replica_groups=mesh['dp'=32,'rep'=4] {'rep'}, use_global_device_ids=true, to_apply=%region_16.17 | all-reduce | flops 8192 | bytes 32768 | tf_op jit(solution)/shard_map/psum | solution.py:100
  272.8 0.6 convert_element_type.127
  273.4 2.6 gather_fusion.1
  276.0 61.1 %reduce-scatter.3.cloned.1.call-done = bf16[512,64]{0,1:T(8,128)(2,1)} async-done(((bf16[512,2048]{0,1:T(8,128)(2,1)}), bf16[512,64]{0,1:T(8,128)(2,1)}) %reduce-scatter.3.cloned.1.call-update) | async-done | bytes 65552 | tf_op jit(solution)/shard_map/reduce_scatter | solution.py:91
  337.2 2.0 broadcast_select_fusion
  339.2 40.8 %all-reduce.6.cloned.1.call-done = bf16[512,64]{0,1:T(8,128)(2,1)} async-done(((bf16[512,64]{0,1:T(8,128)(2,1)}), bf16[512,64]{0,1:T(8,128)(2,1)}) %all-reduce.6.cloned.1.call-update) | async-done | bytes 65552 | tf_op jit(solution)/shard_map/psum | solution.py:99
  379.9 1.5 convert_element_type.124
  (69 shorter events, 0.3 us)
Async XLA Ops:
  7.2 65.4 %copy-start = (bf16[512,2048]{1,0:T(8,128)(2,1)S(1)}, bf16[512,2048]{1,0:T(8,128)(2,1)}, u32[]{:S(2)}) copy-start(bf16[512,2048]{1,0:T(8,128)(2,1)} %param.9) | copy-start | bytes 6291460
  7.2 47.9 %copy-start.1 = (s32[1,512]{1,0:T(1,128)S(1)}, s32[1,512]{1,0:T(1,128)}, u32[]{:S(2)}) copy-start(s32[1,512]{1,0:T(1,128)} %param.13) | copy-start | bytes 6148
  8.0 54.0 %copy-start.21 = (s32[512,1]{0,1:T(1,128)}, s32[512,1]{0,1:T(1,128)S(1)}, u32[]{:S(2)}) copy-start(s32[512,1]{0,1:T(1,128)S(1)} %compare_select_fusion.1) | copy-start | bytes 6148
  12.0 53.0 %all-to-all-start.1 = ((bf16[32,32,512]{2,1,0:T(8,128)(2,1)}), bf16[32,32,512]{2,1,0:T(8,128)(2,1)S(1)}, u32[]{:S(2)}, u32[]{:S(2)}) async-start(bf16[32,32,512]{2,1,0:T(8,128)(2,1)} %bitcast.95), calls=%async_computation.1 | async-start | bytes 2097152 | tf_op jit(solution)/shard_map/all_to_all | solution.py:62
  65.0 13.3 %copy-start.3 = (bf16[32,32,512]{2,1,0:T(8,128)(2,1)}, bf16[32,32,512]{2,1,0:T(8,128)(2,1)S(1)}, u32[]{:S(2)}) copy-start(bf16[32,32,512]{2,1,0:T(8,128)(2,1)S(1)} %all-to-all-done.1) | copy-start | bytes 3145732
  65.0 53.0 %all-to-all-start = ((bf16[32,32,512]{2,1,0:T(8,128)(2,1)}), bf16[32,32,512]{2,1,0:T(8,128)(2,1)}, u32[]{:S(2)}, u32[]{:S(2)}) async-start(bf16[32,32,512]{2,1,0:T(8,128)(2,1)} %bitcast.96), calls=%async_computation | async-start | bytes 2097152 | tf_op jit(solution)/shard_map/all_to_all | solution.py:63
  70.9 184.3 %reduce-scatter.5.cloned.1.call-start = ((), (), s32[]{:S(2)}) async-start(), calls=%async_computation.7 | async-start | bytes 540672 | tf_op jit(solution)/shard_map/reduce_scatter | solution.py:94
  71.6 6.7 %copy-start.15 = (f32[1024]{0:T(1024)}, f32[1024]{0:T(1024)S(1)}, u32[]{:S(2)}) copy-start(f32[1024]{0:T(1024)S(1)} %div.65) | copy-start | bytes 12292
  72.2 6.1 %copy-start.19 = (f32[1024]{0:T(1024)}, f32[1024]{0:T(1024)S(1)}, u32[]{:S(2)}) copy-start(f32[1024]{0:T(1024)S(1)} %add.153) | copy-start | bytes 12292
  72.2 6.1 %copy-start.17 = (f32[1024]{0:T(1024)}, f32[1024]{0:T(1024)S(1)}, u32[]{:S(2)}) copy-start(f32[1024]{0:T(1024)S(1)} %rsqrt.20) | copy-start | bytes 12292
  72.6 5.7 %copy-start.11 = (bf16[1024,512]{1,0:T(8,128)(2,1)}, bf16[1024,512]{1,0:T(8,128)(2,1)S(1)}, u32[]{:S(2)}) copy-start(bf16[1024,512]{1,0:T(8,128)(2,1)S(1)} %multiply_convert_fusion.2) | copy-start | bytes 3145732
  78.3 1.9 copy-start.5
  82.0 21.5 %copy-start.6 = (bf16[1024,512]{0,1:T(8,128)(2,1)}, bf16[1024,512]{0,1:T(8,128)(2,1)S(1)}, u32[]{:S(2)}) copy-start(bf16[1024,512]{0,1:T(8,128)(2,1)S(1)} %get-tuple-element.10) | copy-start | bytes 3145732
  103.5 14.5 %copy-start.14 = (bf16[512,512]{1,0:T(8,128)(2,1)S(1)}, bf16[512,512]{1,0:T(8,128)(2,1)}, u32[]{:S(2)}) copy-start(bf16[512,512]{1,0:T(8,128)(2,1)} %param.10) | copy-start | bytes 1572868
  118.0 10.1 %copy-start.2 = (bf16[8,1024,1024]{2,1,0:T(8,128)(2,1)S(1)}, bf16[8,1024,1024]{2,1,0:T(8,128)(2,1)}, u32[]{:S(2)}) copy-start(bf16[8,1024,1024]{2,1,0:T(8,128)(2,1)} %get-tuple-element.17) | copy-start | bytes 50331652
  128.1 4.0 %copy-start.8 = (f32[1024,1024]{1,0:T(8,128)S(1)}, f32[1024,1024]{1,0:T(8,128)}, u32[]{:S(2)}) copy-start(f32[1024,1024]{1,0:T(8,128)} %fusion.6) | copy-start | bytes 12582916
  128.2 4.0 %copy-start.10 = (bf16[1024,512]{0,1:T(8,128)(2,1)S(1)}, bf16[1024,512]{0,1:T(8,128)(2,1)}, u32[]{:S(2)}) copy-start(bf16[1024,512]{0,1:T(8,128)(2,1)} %get-tuple-element.11) | copy-start | bytes 3145732
  132.2 23.7 %copy-start.13 = (bf16[1024,512]{0,1:T(8,128)(2,1)S(1)}, bf16[1024,512]{0,1:T(8,128)(2,1)}, u32[]{:S(2)}) copy-start(bf16[1024,512]{0,1:T(8,128)(2,1)} %get-tuple-element.9) | copy-start | bytes 3145732
  155.9 9.9 %copy-start.7 = (bf16[1024,512]{0,1:T(8,128)(2,1)S(1)}, bf16[1024,512]{0,1:T(8,128)(2,1)}, u32[]{:S(2)}) copy-start(bf16[1024,512]{0,1:T(8,128)(2,1)} %copy-done.6) | copy-start | bytes 3145732
  176.1 161.1 %reduce-scatter.3.cloned.1.call-start = ((), (), s32[]{:S(2)}) async-start(), calls=%async_computation.5 | async-start | bytes 2162688 | tf_op jit(solution)/shard_map/reduce_scatter | solution.py:91
  176.1 8.3 %copy-start.12 = (bf16[1024,512]{1,0:T(8,128)(2,1)S(1)}, bf16[1024,512]{1,0:T(8,128)(2,1)}, u32[]{:S(2)}) copy-start(bf16[1024,512]{1,0:T(8,128)(2,1)} %copy-done.11) | copy-start | bytes 3145732
  182.5 1.9 copy-start.9
  184.4 3.7 copy-start.4
  184.4 3.7 copy-start.16
  188.2 4.9 %copy-start.20 = (f32[1024]{0:T(1024)S(1)}, f32[1024]{0:T(1024)}, u32[]{:S(2)}) copy-start(f32[1024]{0:T(1024)} %copy-done.19) | copy-start | bytes 12292
  188.2 4.9 %copy-start.18 = (f32[1024]{0:T(1024)S(1)}, f32[1024]{0:T(1024)}, u32[]{:S(2)}) copy-start(f32[1024]{0:T(1024)} %copy-done.17) | copy-start | bytes 12292
  193.1 11.3 %copy-start.22 = (s32[512,1]{0,1:T(1,128)S(1)}, s32[512,1]{0,1:T(1,128)}, u32[]{:S(2)}) copy-start(s32[512,1]{0,1:T(1,128)} %copy-done.21) | copy-start | bytes 6148
  193.1 11.3 %copy-start.23 = (s32[1,512]{1,0:T(1,128)S(1)}, s32[1,512]{1,0:T(1,128)}, u32[]{:S(2)}) copy-start(s32[1,512]{1,0:T(1,128)} %param.11) | copy-start | bytes 6148
  197.0 76.4 %all-to-all-start.2 = ((bf16[32,32,512]{2,1,0:T(8,128)(2,1)}), bf16[32,32,512]{2,1,0:T(8,128)(2,1)S(1)}, u32[]{:S(2)}, u32[]{:S(2)}) async-start(bf16[32,32,512]{2,1,0:T(8,128)(2,1)} %bitcast.97), calls=%async_computation.2 | async-start | bytes 2097152 | tf_op jit(solution)/shard_map/all_to_all | solution.py:86
  204.3 175.6 %all-reduce.6.cloned.1.call-start = ((), (), s32[]{:S(2)}) async-start(), calls=%async_computation.6 | async-start | bytes 131072 | tf_op jit(solution)/shard_map/psum | solution.py:99
Sparse Core Ops, SparseCore 0:
  176.2 79.0 reduce-scatter.4
  258.8 78.2 reduce-scatter.2
  339.5 40.4 all-reduce.5
where the time goes:
time: 395 us; the launch traced here: 388 us
  waiting for transfers between devices  153 us (39%)
  matrix products  99.4 us (25%)
  blocking collectives  47.3 us (12%)
  other arithmetic  28.3 us (7%)
  local copies, waits for them, and re-layouts  24 us (6%)
  starting transfers between devices  22 us (6%)
  between operations  14.4 us (4%)
    reduce_scatter x1, waiting for transfers between devices, on_device(): lax.psum_scatter(grad_in.astype(jnp.bfloat16), 'dp', scatter_dimension=1,...  61.1 us
    reduce_scatter x1, waiting for transfers between devices, on_device(): lax.psum_scatter(grad_outw.astype(jnp.bfloat16), 'dp', scatter_dimension=...  50.9 us
    psum x1, waiting for transfers between devices, on_device(): lax.psum(part_in.astype(jnp.bfloat16), 'rep').astype(jnp.float32)  40.8 us
    dot_general x3, matrix products, hstu_layer(): jnp.einsum('hqk,khd->qhd', weights, values, preferred_element_type=jnp.fl...  40.4 us
    dot_general x3, matrix products, hstu_layer(): jnp.einsum('qhd,khd->hqk', queries, keys, preferred_element_type=jnp.floa...  38.8 us
    all_gather x1, blocking collectives, on_device(): count_table = lax.all_gather(send_counts, 'dp', axis=0, tiled=True)  29.8 us
    psum x1, blocking collectives, on_device(): lax.psum(part_out.astype(jnp.bfloat16), 'rep').astype(jnp.float32)  17.5 us
    dot_general x3, matrix products, hstu_layer(): jnp.dot(normalized_input, input_weight_matrix, preferred_element_type=jnp...  14.3 us
  transfers between devices with their start and end apart: 6, of which 3 were waited for; matrix products, arithmetic and copies ran while one was open for 22% of the time, Pallas kernels for 0%

commit v1 on v0

--- a/solution.py
+++ b/solution.py
@@ -96,7 +96,9 @@
         ).astype(jnp.float32),
     )
     share_in, share_out = (
-        lax.psum(part_in.astype(jnp.bfloat16), "rep").astype(jnp.float32),
+        jnp.sum(lax.all_gather(part_in.astype(jnp.bfloat16), axis_name="rep"), axis=0).astype(
+            jnp.float32
+        ),
         lax.psum(part_out.astype(jnp.bfloat16), "rep").astype(jnp.float32),
     )
     return (grad_events, share_in, share_out)

time: 395 us -> 365 us (0.924)
  waiting for transfers between devices: 153 us -> 110 us
  blocking collectives: 47.3 us -> 60.1 us
    psum x1 -> x0, waiting for transfers between devices: 40.8 us -> none  [on_device(): lax.psum(part_in.astype(jnp.bfloat16), 'rep').astype(jnp.float32)]
    all_gather x0 -> x1, blocking collectives: none -> 12.9 us  [on_device(): lax.all_gather(part_in.astype(jnp.bfloat16), axis_name='rep')]
  transfers between devices with their start and end apart: 6 -> 5, of which waited for: 3 -> 2; matrix products, arithmetic and copies ran while one was open for 22% -> 23% of each run, Pallas kernels for 0% -> 0%
where the time goes in v1:
time: 365 us; the launch traced here: 358 us
  waiting for transfers between devices  110 us (30%)
  matrix products  99.4 us (27%)
  blocking collectives  60.1 us (16%)
  other arithmetic  27.8 us (8%)
  local copies, waits for them, and re-layouts  24.2 us (7%)
  starting transfers between devices  21.9 us (6%)
  between operations  14.7 us (4%)
    reduce_scatter x1, waiting for transfers between devices, on_device(): lax.psum_scatter(grad_in.astype(jnp.bfloat16), 'dp', scatter_dimension=1,...  59.2 us
    reduce_scatter x1, waiting for transfers between devices, on_device(): lax.psum_scatter(grad_outw.astype(jnp.bfloat16), 'dp', scatter_dimension=...  50.9 us
    dot_general x3, matrix products, hstu_layer(): jnp.einsum('hqk,khd->qhd', weights, values, preferred_element_type=jnp.fl...  40.4 us
    dot_general x3, matrix products, hstu_layer(): jnp.einsum('qhd,khd->hqk', queries, keys, preferred_element_type=jnp.floa...  38.8 us
    all_gather x1, blocking collectives, on_device(): count_table = lax.all_gather(send_counts, 'dp', axis=0, tiled=True)  29.8 us
    psum x1, blocking collectives, on_device(): lax.psum(part_out.astype(jnp.bfloat16), 'rep').astype(jnp.float32)  17.5 us
    dot_general x3, matrix products, hstu_layer(): jnp.dot(normalized_input, input_weight_matrix, preferred_element_type=jnp...  14.3 us
    all_gather x1, blocking collectives, on_device(): lax.all_gather(part_in.astype(jnp.bfloat16), axis_name='rep')  12.9 us
  transfers between devices with their start and end apart: 5, of which 2 were waited for; matrix products, arithmetic and copies ran while one was open for 23% of the time, Pallas kernels for 0%

profile of v1, /device:TPU:0, one launch (start us, length us, event | category | flops | bytes accessed | tf_op | source)
XLA Modules:
  0.0 358.3 jit_solution(13566527694663402966)
XLA Ops:
  7.2 0.8 compare_select_fusion.1
  8.0 4.0 %scatter_custom_fusion.1 = bf16[1024,512]{1,0:T(8,128)(2,1)} fusion(s32[512]{0:T(512)S(1)} %bitcast.108, bf16[512,512]{1,0:T(8,128)(2,1)} %param.7, bf16[]{:T(256)} %constant.84.clone.1), kind=kCustom, calls=%fused_computation.50 | custom fusion | bytes 1049088 | tf_op jit(solution)/shard_map/scatter | solution.py:59
  12.0 8.3 %all-to-all-start.1 = ((bf16[32,32,512]{2,1,0:T(8,128)(2,1)}), bf16[32,32,512]{2,1,0:T(8,128)(2,1)S(1)}, u32[]{:S(2)}, u32[]{:S(2)}) async-start(bf16[32,32,512]{2,1,0:T(8,128)(2,1)} %bitcast.97), calls=%async_computation.1 | async-start | bytes 2097152 | tf_op jit(solution)/shard_map/all_to_all | solution.py:62
  20.3 29.8 %all-gather.1 = s32[32,1,32]{2,1,0:T(1,128)S(1)} all-gather(s32[1,1,32]{2,1,0:T(1,128)} %bitcast.112), channel_id=1, replica_groups=mesh['dp'=32,'rep'=4] {'dp'}, dimensions={0}, use_global_device_ids=true | all-gather | bytes 4224 | tf_op jit(solution)/shard_map/all_gather | solution.py:65
  50.1 0.7 fusion.27
  50.9 0.1 reduce.7
  51.0 0.1 select_reduce_fusion.1
  51.1 4.0 %scatter_custom_fusion = bf16[1024,512]{1,0:T(8,128)(2,1)} fusion(s32[512]{0:T(512)S(1)} %bitcast.109, bf16[512,512]{1,0:T(8,128)(2,1)} %param.8, bf16[]{:T(256)} %constant.84.clone.1), kind=kCustom, calls=%fused_computation.52 | custom fusion | bytes 1049088 | tf_op jit(solution)/shard_map/scatter | solution.py:60
  55.1 6.9 %gather_fusion = s32[1024]{0:T(1024)S(1)} fusion(s32[512]{0:T(512)S(1)} %bitcast.89, s32[1024]{0:T(1024)S(1)} %broadcast_clamp_fusion), kind=kCustom, calls=%fused_computation | custom fusion | bytes 12288 | tf_op jit(solution)/shard_map/jit(_take)/gather | solution.py:78
  62.0 2.9 fusion.6
  65.0 6.0 %all-to-all-start = ((bf16[32,32,512]{2,1,0:T(8,128)(2,1)}), bf16[32,32,512]{2,1,0:T(8,128)(2,1)}, u32[]{:S(2)}, u32[]{:S(2)}) async-start(bf16[32,32,512]{2,1,0:T(8,128)(2,1)} %bitcast.98), calls=%async_computation | async-start | bytes 2097152 | tf_op jit(solution)/shard_map/all_to_all | solution.py:63
  70.9 0.3 reduce-scatter.5.cloned.1.call-start
  71.3 0.2 convert_reduce_fusion
  71.5 0.1 div.65
  71.6 0.5 multiply_reduce_fusion.1
  72.1 0.1 add.151
  72.2 0.3 multiply_convert_fusion.2
  72.6 5.7 %multiply_convert_fusion.1 = (bf16[1024,2048]{0,1:T(8,128)(2,1)S(1)}, f32[1024,2048]{0,1:T(8,128)}) fusion(bf16[1024,512]{1,0:T(8,128)(2,1)S(1)} %multiply_convert_fusion.2, bf16[512,2048]{1,0:T(8,128)(2,1)S(1)} %copy-done), kind=kOutput, calls=%fused_computation.15 | convolution fusion | flops 2157969408 | bytes 15728640 | tf_op jit(solution)/shard_map/jvp()/dot_general | solution.py:24
  78.3 1.9 copy-done.5
  80.2 1.8 fusion.28
  82.0 21.5 %multiply_convert_fusion = (bf16[8,1024,1024]{2,1,0:T(8,128)(2,1)}, f32[8,1024,1024]{2,1,0:T(8,128)}) fusion(f32[1024,1024]{1,0:T(8,128)} %fusion.6, bf16[1024,8,64]{0,2,1:T(8,128)(2,1)S(1)} %bitcast.92, bf16[1024,8,64]{0,2,1:T(8,128)(2,1)} %bitcast.103), kind=kOutput, calls=%fused_computation.8 | convolution fusion | flops 1132462080 | bytes 56623104 | tf_op jit(solution)/shard_map/jvp(qhd,khd->hqk)/dot_general | solution.py:30
  103.5 12.7 %fusion.29 = (f32[1024]{0:T(1024)S(1)}, f32[8,64,1024]{2,1,0:T(8,128)}) fusion(bf16[1024,8,64]{0,2,1:T(8,128)(2,1)} %bitcast.100, bf16[8,1024,1024]{2,1,0:T(8,128)(2,1)} %get-tuple-element.17), kind=kOutput, calls=%fused_computation.96 | convolution fusion | flops 1074265088 | bytes 19927040 | tf_op jit(solution)/shard_map/jvp(hqk,khd->qhd)/dot_general | solution.py:34
  116.1 1.8 fusion.11
  118.0 3.2 multiply_reduce_fusion
  121.2 4.4 %fusion.8 = (bf16[1024,512]{0,1:T(8,128)(2,1)S(1)}, f32[1024]{0:T(1024)S(1)}, bf16[1024,512]{0,1:T(8,128)(2,1)}) fusion(f32[8,64,1024]{2,1,0:T(8,128)} %get-tuple-element.20, f32[1024]{0:T(1024)S(1)} %broadcast_multiply_fusion.1, f32[1024]{0:T(1024)S(1)} %get-tuple-element.14, bf16[1024,2048]{0,1:T(8,128)(2,1)} %copy-done.5, f32[1024]{0:T(1024)S(1)} %get-tuple-element.13, ...), kind=kLoop, calls=%fused_computation.29 | loop fusion | flops 7339008 | bytes 6307840 | tf_op jit(solution)/shard_map/jvp()/convert_element_type | solution.py:37
  125.6 2.6 broadcast_add_fusion
  128.2 4.0 %fusion.33 = bf16[8,64,1024]{2,1,0:T(8,128)(2,1)} fusion(bf16[8,64,1024]{2,1,0:T(8,128)(2,1)S(1)} %bitcast.95, bf16[8,1024,1024]{2,1,0:T(8,128)(2,1)S(1)} %copy-done.2), kind=kOutput, calls=%fused_computation.100 | convolution fusion | flops 1073741824 | bytes 18874368 | tf_op jit(solution)/shard_map/transpose(jvp(hqk,khd->qhd))/dot_general | solution.py:34
  132.2 23.7 %fusion.2 = bf16[8,1024,1024]{2,1,0:T(8,128)(2,1)} fusion(f32[8,1024,1024]{2,1,0:T(8,128)} %get-tuple-element.18, f32[1024,1024]{1,0:T(8,128)S(1)} %copy-done.8, bf16[8,64,1024]{2,1,0:T(8,128)(2,1)S(1)} %bitcast.96, bf16[1024,8,64]{0,2,1:T(8,128)(2,1)S(1)} %bitcast.101), kind=kOutput, calls=%fused_computation.7 | convolution fusion | flops 1191182336 | bytes 56623104 | tf_op jit(solution)/shard_map/transpose(jvp(hqk,khd->qhd))/dot_general | solution.py:34
  155.9 9.8 %fusion.31 = bf16[8,1024,64]{1,2,0:T(8,128)(2,1)} fusion(bf16[8,1024,1024]{2,1,0:T(8,128)(2,1)} %fusion.2, bf16[1024,8,64]{0,2,1:T(8,128)(2,1)S(1)} %bitcast.104), kind=kOutput, calls=%fused_computation.98 | convolution fusion | flops 1073741824 | bytes 18874368 | tf_op jit(solution)/shard_map/transpose(jvp(qhd,khd->hqk))/dot_general | solution.py:30
  165.8 7.5 %fusion.32 = bf16[8,1024,64]{1,2,0:T(8,128)(2,1)S(1)} fusion(bf16[8,1024,1024]{2,1,0:T(8,128)(2,1)} %fusion.2, bf16[1024,8,64]{0,2,1:T(8,128)(2,1)S(1)} %bitcast.93), kind=kOutput, calls=%fused_computation.99 | convolution fusion | flops 1073741824 | bytes 18874368 | tf_op jit(solution)/shard_map/transpose(jvp(qhd,khd->hqk))/dot_general | solution.py:30
  173.2 2.8 convolution_convert_fusion.6
  176.1 6.4 %fusion.3 = bf16[1024,2048]{0,1:T(8,128)(2,1)S(1)} fusion(f32[1024,2048]{0,1:T(8,128)} %get-tuple-element.16, bf16[1024,512]{0,1:T(8,128)(2,1)} %get-tuple-element.12, bf16[1024,512]{0,1:T(8,128)(2,1)} %bitcast.94, bf16[1024,512]{0,1:T(8,128)(2,1)} %bitcast.102, bf16[1024,512]{0,1:T(8,128)(2,1)S(1)} %bitcast.91), kind=kLoop, calls=%fused_computation.13 | loop fusion | flops 37748736 | bytes 16777216 | tf_op jit(solution)/shard_map/transpose(jvp(jit(silu)))/add_any | solution.py:23
  182.5 1.9 copy-done.9
  184.4 3.7 %fusion.30 = bf16[512,2048]{0,1:T(8,128)(2,1)} fusion(bf16[1024,512]{1,0:T(8,128)(2,1)S(1)} %copy-done.12, bf16[1024,2048]{0,1:T(8,128)(2,1)S(1)} %fusion.3), kind=kOutput, calls=%fused_computation.97 | convolution fusion | flops 2147483648 | bytes 7340032 | tf_op jit(solution)/shard_map/transpose(jvp())/dot_general | solution.py:24
  188.2 4.9 %fusion.9 = (f32[1024]{0:T(1024)S(1)}, bf16[1024,512]{1,0:T(8,128)(2,1)S(1)}) fusion(bf16[32,32,512]{2,1,0:T(8,128)(2,1)S(1)} %copy-done.4, f32[1024]{0:T(1024)S(1)} %copy-done.16, bf16[1024,2048]{0,1:T(8,128)(2,1)} %copy-done.9, bf16[512,2048]{1,0:T(8,128)(2,1)S(1)} %copy-done), kind=kOutput, calls=%fused_computation.30 | convolution fusion | flops 2150104064 | bytes 8396800 | tf_op jit(solution)/shard_map/transpose(jvp())/dot_general | solution.py:24
  193.1 1.0 fusion.12
  194.2 2.8 fusion.13
  197.0 7.3 %all-to-all-start.2 = ((bf16[32,32,512]{2,1,0:T(8,128)(2,1)}), bf16[32,32,512]{2,1,0:T(8,128)(2,1)S(1)}, u32[]{:S(2)}, u32[]{:S(2)}) async-start(bf16[32,32,512]{2,1,0:T(8,128)(2,1)} %bitcast.99), calls=%async_computation.2 | async-start | bytes 2097152 | tf_op jit(solution)/shard_map/all_to_all | solution.py:86
  204.4 50.9 %reduce-scatter.5.cloned.1.call-done = bf16[512,16]{0,1:T(8,128)(2,1)} async-done(((bf16[512,512]{0,1:T(8,128)(2,1)}), bf16[512,16]{0,1:T(8,128)(2,1)}) %reduce-scatter.5.cloned.1.call-update) | async-done | bytes 16400 | tf_op jit(solution)/shard_map/reduce_scatter | solution.py:94
  255.3 17.5 %psum.7 = bf16[512,16]{0,1:T(8,128)(2,1)S(1)} all-reduce(bf16[512,16]{0,1:T(8,128)(2,1)} %reduce-scatter.5.cloned.1.call-done), channel_id=1, replica_groups=mesh['dp'=32,'rep'=4] {'rep'}, use_global_device_ids=true, to_apply=%region_16.17 | all-reduce | flops 8192 | bytes 32768 | tf_op jit(solution)/shard_map/psum | solution.py:102
  272.8 0.6 convert_element_type.129
  273.4 2.6 gather_fusion.1
  276.0 2.0 broadcast_select_fusion
  278.0 59.2 %reduce-scatter.3.cloned.1.call-done = bf16[512,64]{0,1:T(8,128)(2,1)} async-done(((bf16[512,2048]{0,1:T(8,128)(2,1)}), bf16[512,64]{0,1:T(8,128)(2,1)}) %reduce-scatter.3.cloned.1.call-update) | async-done | bytes 65552 | tf_op jit(solution)/shard_map/reduce_scatter | solution.py:91
  337.2 12.9 %all-gather = bf16[2048,64]{0,1:T(8,128)(2,1)S(1)} all-gather(bf16[512,64]{0,1:T(8,128)(2,1)} %reduce-scatter.3.cloned.1.call-done), channel_id=2, replica_groups=mesh['dp'=32,'rep'=4] {'rep'}, dimensions={0}, use_global_device_ids=true | all-gather | bytes 327680 | tf_op jit(solution)/shard_map/all_gather | solution.py:99
  350.0 0.2 reshape.402
  350.2 0.3 reduce_sum.131
  350.5 0.7 convert_element_type.126
  (69 shorter events, 0.3 us)
Async XLA Ops:
  7.2 65.4 %copy-start = (bf16[512,2048]{1,0:T(8,128)(2,1)S(1)}, bf16[512,2048]{1,0:T(8,128)(2,1)}, u32[]{:S(2)}) copy-start(bf16[512,2048]{1,0:T(8,128)(2,1)} %param.9) | copy-start | bytes 6291460
  7.2 47.9 %copy-start.1 = (s32[1,512]{1,0:T(1,128)S(1)}, s32[1,512]{1,0:T(1,128)}, u32[]{:S(2)}) copy-start(s32[1,512]{1,0:T(1,128)} %param.13) | copy-start | bytes 6148
  8.0 54.0 %copy-start.21 = (s32[512,1]{0,1:T(1,128)}, s32[512,1]{0,1:T(1,128)S(1)}, u32[]{:S(2)}) copy-start(s32[512,1]{0,1:T(1,128)S(1)} %compare_select_fusion.1) | copy-start | bytes 6148
  12.0 53.0 %all-to-all-start.1 = ((bf16[32,32,512]{2,1,0:T(8,128)(2,1)}), bf16[32,32,512]{2,1,0:T(8,128)(2,1)S(1)}, u32[]{:S(2)}, u32[]{:S(2)}) async-start(bf16[32,32,512]{2,1,0:T(8,128)(2,1)} %bitcast.97), calls=%async_computation.1 | async-start | bytes 2097152 | tf_op jit(solution)/shard_map/all_to_all | solution.py:62
  65.0 13.3 %copy-start.3 = (bf16[32,32,512]{2,1,0:T(8,128)(2,1)}, bf16[32,32,512]{2,1,0:T(8,128)(2,1)S(1)}, u32[]{:S(2)}) copy-start(bf16[32,32,512]{2,1,0:T(8,128)(2,1)S(1)} %all-to-all-done.1) | copy-start | bytes 3145732
  65.0 53.0 %all-to-all-start = ((bf16[32,32,512]{2,1,0:T(8,128)(2,1)}), bf16[32,32,512]{2,1,0:T(8,128)(2,1)}, u32[]{:S(2)}, u32[]{:S(2)}) async-start(bf16[32,32,512]{2,1,0:T(8,128)(2,1)} %bitcast.98), calls=%async_computation | async-start | bytes 2097152 | tf_op jit(solution)/shard_map/all_to_all | solution.py:63
  70.9 184.3 %reduce-scatter.5.cloned.1.call-start = ((), (), s32[]{:S(2)}) async-start(), calls=%async_computation.6 | async-start | bytes 540672 | tf_op jit(solution)/shard_map/reduce_scatter | solution.py:94
  71.6 6.7 %copy-start.15 = (f32[1024]{0:T(1024)}, f32[1024]{0:T(1024)S(1)}, u32[]{:S(2)}) copy-start(f32[1024]{0:T(1024)S(1)} %div.65) | copy-start | bytes 12292
  72.2 6.1 %copy-start.19 = (f32[1024]{0:T(1024)}, f32[1024]{0:T(1024)S(1)}, u32[]{:S(2)}) copy-start(f32[1024]{0:T(1024)S(1)} %add.151) | copy-start | bytes 12292
  72.2 6.1 %copy-start.17 = (f32[1024]{0:T(1024)}, f32[1024]{0:T(1024)S(1)}, u32[]{:S(2)}) copy-start(f32[1024]{0:T(1024)S(1)} %rsqrt.20) | copy-start | bytes 12292
  72.6 5.7 %copy-start.11 = (bf16[1024,512]{1,0:T(8,128)(2,1)}, bf16[1024,512]{1,0:T(8,128)(2,1)S(1)}, u32[]{:S(2)}) copy-start(bf16[1024,512]{1,0:T(8,128)(2,1)S(1)} %multiply_convert_fusion.2) | copy-start | bytes 3145732
  78.3 1.9 copy-start.5
  82.0 21.5 %copy-start.6 = (bf16[1024,512]{0,1:T(8,128)(2,1)}, bf16[1024,512]{0,1:T(8,128)(2,1)S(1)}, u32[]{:S(2)}) copy-start(bf16[1024,512]{0,1:T(8,128)(2,1)S(1)} %get-tuple-element.10) | copy-start | bytes 3145732
  103.5 14.5 %copy-start.14 = (bf16[512,512]{1,0:T(8,128)(2,1)S(1)}, bf16[512,512]{1,0:T(8,128)(2,1)}, u32[]{:S(2)}) copy-start(bf16[512,512]{1,0:T(8,128)(2,1)} %param.10) | copy-start | bytes 1572868
  118.0 10.1 %copy-start.2 = (bf16[8,1024,1024]{2,1,0:T(8,128)(2,1)S(1)}, bf16[8,1024,1024]{2,1,0:T(8,128)(2,1)}, u32[]{:S(2)}) copy-start(bf16[8,1024,1024]{2,1,0:T(8,128)(2,1)} %get-tuple-element.17) | copy-start | bytes 50331652
  128.1 4.0 %copy-start.8 = (f32[1024,1024]{1,0:T(8,128)S(1)}, f32[1024,1024]{1,0:T(8,128)}, u32[]{:S(2)}) copy-start(f32[1024,1024]{1,0:T(8,128)} %fusion.6) | copy-start | bytes 12582916
  128.2 4.0 %copy-start.10 = (bf16[1024,512]{0,1:T(8,128)(2,1)S(1)}, bf16[1024,512]{0,1:T(8,128)(2,1)}, u32[]{:S(2)}) copy-start(bf16[1024,512]{0,1:T(8,128)(2,1)} %get-tuple-element.11) | copy-start | bytes 3145732
  132.2 23.7 %copy-start.13 = (bf16[1024,512]{0,1:T(8,128)(2,1)S(1)}, bf16[1024,512]{0,1:T(8,128)(2,1)}, u32[]{:S(2)}) copy-start(bf16[1024,512]{0,1:T(8,128)(2,1)} %get-tuple-element.9) | copy-start | bytes 3145732
  155.9 9.9 %copy-start.7 = (bf16[1024,512]{0,1:T(8,128)(2,1)S(1)}, bf16[1024,512]{0,1:T(8,128)(2,1)}, u32[]{:S(2)}) copy-start(bf16[1024,512]{0,1:T(8,128)(2,1)} %copy-done.6) | copy-start | bytes 3145732
  176.1 161.1 %reduce-scatter.3.cloned.1.call-start = ((), (), s32[]{:S(2)}) async-start(), calls=%async_computation.5 | async-start | bytes 2162688 | tf_op jit(solution)/shard_map/reduce_scatter | solution.py:91
  176.1 8.3 %copy-start.12 = (bf16[1024,512]{1,0:T(8,128)(2,1)S(1)}, bf16[1024,512]{1,0:T(8,128)(2,1)}, u32[]{:S(2)}) copy-start(bf16[1024,512]{1,0:T(8,128)(2,1)} %copy-done.11) | copy-start | bytes 3145732
  182.5 1.9 copy-start.9
  184.4 3.7 %copy-start.4 = (bf16[32,32,512]{2,1,0:T(8,128)(2,1)S(1)}, bf16[32,32,512]{2,1,0:T(8,128)(2,1)}, u32[]{:S(2)}) copy-start(bf16[32,32,512]{2,1,0:T(8,128)(2,1)} %copy-done.3) | copy-start | bytes 3145732
  184.4 3.7 %copy-start.16 = (f32[1024]{0:T(1024)S(1)}, f32[1024]{0:T(1024)}, u32[]{:S(2)}) copy-start(f32[1024]{0:T(1024)} %copy-done.15) | copy-start | bytes 12292
  188.2 4.9 %copy-start.20 = (f32[1024]{0:T(1024)S(1)}, f32[1024]{0:T(1024)}, u32[]{:S(2)}) copy-start(f32[1024]{0:T(1024)} %copy-done.19) | copy-start | bytes 12292
  188.2 4.9 %copy-start.18 = (f32[1024]{0:T(1024)S(1)}, f32[1024]{0:T(1024)}, u32[]{:S(2)}) copy-start(f32[1024]{0:T(1024)} %copy-done.17) | copy-start | bytes 12292
  193.1 11.2 %copy-start.22 = (s32[512,1]{0,1:T(1,128)S(1)}, s32[512,1]{0,1:T(1,128)}, u32[]{:S(2)}) copy-start(s32[512,1]{0,1:T(1,128)} %copy-done.21) | copy-start | bytes 6148
  193.1 11.2 %copy-start.23 = (s32[1,512]{1,0:T(1,128)S(1)}, s32[1,512]{1,0:T(1,128)}, u32[]{:S(2)}) copy-start(s32[1,512]{1,0:T(1,128)} %param.11) | copy-start | bytes 6148
  197.0 76.4 %all-to-all-start.2 = ((bf16[32,32,512]{2,1,0:T(8,128)(2,1)}), bf16[32,32,512]{2,1,0:T(8,128)(2,1)S(1)}, u32[]{:S(2)}, u32[]{:S(2)}) async-start(bf16[32,32,512]{2,1,0:T(8,128)(2,1)} %bitcast.99), calls=%async_computation.2 | async-start | bytes 2097152 | tf_op jit(solution)/shard_map/all_to_all | solution.py:86
Sparse Core Ops, SparseCore 0:
  176.2 79.0 reduce-scatter.4
  258.8 78.2 reduce-scatter.2
